TPU v7x, 32 devices: a whole 2x2x4 slice. The times are simulated.
32 devices in a mesh: grp: 8 (over y, x, core), seq: 4 (over z).
Axes of the slice: x: 2, y: 2, z: 4, core: 2. Of those that a mesh axis runs over, the one named last changes fastest.
Arguments:
- tokens: bfloat16 [8192, 2048], P(('grp', 'seq')), may hold values from -6 to 6
- cotangent: bfloat16 [8192, 2048], P(('grp', 'seq')), may hold values from -6 to 6
- segment_ids: int32 [8192], P(('grp', 'seq')), may hold values from 0 to 31, never falling along the last dimension, each value on 1 to 768 neighbouring positions
- tile_owner_slots: int32 [166], replicated, may hold values from 0 to 167, as said below
- weights_low: bfloat16 [168, 2048, 128], P('grp', 'seq')
- master: float32 [168, 2048, 128], P('grp', 'seq')
- moment_one: float32 [168, 2048, 128], P('grp', 'seq')
- moment_two: float32 [168, 2048, 128], P('grp', 'seq'), as said below
- left_basis_set: float32 [168, 2048, 512], P('grp', 'seq'), as said below
- right_basis_set: float32 [168, 512, 128], P('grp', 'seq'), as said below
- gains: float32 [2, 2048], replicated, may hold values from 0.5 to 1.5
- gain_moment_one: float32 [2, 2048], replicated, may hold values from -28 to 28
- gain_moment_two: float32 [2, 2048], replicated, may hold values from 430.8992 to 1720.32
Outputs:
- block_out: bfloat16 [8192, 2048], P(('grp', 'seq'))
- input_grad: float32 [8192, 2048], P(('grp', 'seq'))
- new_master: float32 [168, 2048, 128], P('grp', 'seq')
- new_moment_one: float32 [168, 2048, 128], P('grp', 'seq')
- new_moment_two: float32 [168, 2048, 128], P('grp', 'seq')
- gain_grads: float32 [2, 2048], replicated
- new_gains: float32 [2, 2048], replicated
- new_gain_one: float32 [2, 2048], replicated
- new_gain_two: float32 [2, 2048], replicated
Inputs may be any that keep to these rules, and one draw needn't show every extreme that they name: `tile_owner_slots`: the entries are distinct; slot q belongs to data group q // 21. `segment_ids`: never falls along the tokens. `left_basis_set`: each 512 x 512 block is orthogonal. `right_basis_set`: each 128 x 128 block is orthogonal. `moment_two`: positive.
All inputs are finite; a program needn't handle non-finite values.
Results may differ from a plain program's by a relative error of at most 0.015.
Values may be sent and summed in bfloat16 or wider, within the bound.
A program may use at most 704 MiB of HBM per device.

v0:
```python
import jax
import jax.numpy as jnp
from jax import lax
from jax.sharding import PartitionSpec as P

MODEL_WIDTH = 2048
NH = 16
HD = 128
FF = 5632
SEQLEN = 1024
NORM_EPS = 1e-05
BETA_ONE = 0.95
BETA_TWO = 0.95
ADAM_EPS = 1e-08
WEIGHT_DECAY = 0.01
LEARN_RATE = 0.03
GAIN_RATE = 1.5
ROPE_BASE = 10000.0
MASKED = -1e30
PRECISE = lax.Precision.HIGHEST


def rotate(values, positions, direction):
    head_width = values.shape[-1]
    half_width = head_width // 2
    frequency = ROPE_BASE ** (-(jnp.arange(half_width, dtype=jnp.float32) * 2.0) / head_width)
    angles = positions.astype(jnp.float32)[:, None] * frequency[None, :]
    cosine = jnp.cos(angles)[:, None, :]
    sine_part = (jnp.sin(angles) * direction)[:, None, :]
    leading = values[..., :half_width]
    trailing = values[..., half_width:]
    return jnp.concatenate(
        [leading * cosine - trailing * sine_part, trailing * cosine + leading * sine_part], axis=-1
    )


def visible(query_index, key_index, query_seg, key_seg):
    causal = query_index[:, None] >= key_index[None, :]
    same_seq = query_index[:, None] // SEQLEN == key_index[None, :] // SEQLEN
    same_doc = query_seg[:, None] == key_seg[None, :]
    return causal & same_seq & same_doc


def contract(left_side, right_side):
    return lax.dot_general(
        left_side, right_side, (((0,), (0,)), ((), ())), preferred_element_type=jnp.float32
    )


def times_transpose(left_side, right_side):
    return lax.dot_general(
        left_side, right_side, (((1,), (1,)), ((), ())), preferred_element_type=jnp.float32
    )


def attend(queries, key_rows, value_rows, query_index, query_seg, key_index, key_seg):
    query_total, head_count, head_width = queries.shape
    block_rows = min(512, query_total)
    block_count = query_total // block_rows
    score_scale = head_width ** (-0.5)

    def one_block(inputs):
        block_queries, block_index, block_seg = inputs
        raw_scores = jnp.einsum(
            "qhd,kd->hqk", block_queries, key_rows, preferred_element_type=jnp.float32
        )
        allowed = visible(block_index, key_index, block_seg, key_seg)
        score_matrix = jnp.where(allowed[None], raw_scores * score_scale, MASKED)
        highest = jnp.max(score_matrix, axis=-1, keepdims=True)
        exponent = jnp.exp(score_matrix - highest)
        totals = jnp.sum(exponent, axis=-1, keepdims=True)
        probs_low = (exponent / totals).astype(jnp.bfloat16)
        context = jnp.einsum(
            "hqk,kd->qhd", probs_low, value_rows, preferred_element_type=jnp.float32
        )
        return (context, jnp.transpose((highest + jnp.log(totals))[..., 0]))

    context, log_totals = lax.map(
        one_block,
        (
            queries.reshape(block_count, block_rows, head_count, head_width),
            query_index.reshape(block_count, block_rows),
            query_seg.reshape(block_count, block_rows),
        ),
    )
    return (
        context.reshape(query_total, head_count, head_width),
        log_totals.reshape(query_total, head_count),
    )


def attend_back(
    queries, key_rows, value_rows, grads_low, log_totals, query_index, query_seg, key_index, key_seg
):
    query_total, head_count, head_width = queries.shape
    block_rows = min(512, query_total)
    block_count = query_total // block_rows
    score_scale = head_width ** (-0.5)

    def one_block(running, inputs):
        block_queries, block_grads, block_totals, block_index, block_seg = inputs
        raw_scores = jnp.einsum(
            "qhd,kd->hqk", block_queries, key_rows, preferred_element_type=jnp.float32
        )
        allowed = visible(block_index, key_index, block_seg, key_seg)
        shifted = raw_scores * score_scale - jnp.transpose(block_totals)[:, :, None]
        probs = jnp.where(allowed[None], jnp.exp(shifted), 0.0)
        prob_grad = jnp.einsum(
            "qhd,kd->hqk", block_grads, value_rows, preferred_element_type=jnp.float32
        )
        centre = jnp.sum(probs * prob_grad, axis=-1, keepdims=True)
        score_grad = (probs * (prob_grad - centre) * score_scale).astype(jnp.bfloat16)
        query_part = jnp.einsum(
            "hqk,kd->qhd", score_grad, key_rows, preferred_element_type=jnp.float32
        )
        key_part = running[0] + jnp.einsum(
            "hqk,qhd->kd", score_grad, block_queries, preferred_element_type=jnp.float32
        )
        value_part = running[1] + jnp.einsum(
            "hqk,qhd->kd",
            probs.astype(jnp.bfloat16),
            block_grads,
            preferred_element_type=jnp.float32,
        )
        return ((key_part, value_part), query_part)

    zeros_rows = jnp.zeros(key_rows.shape, jnp.float32)
    (key_grad, value_grad), query_grad = lax.scan(
        one_block,
        (zeros_rows, zeros_rows),
        (
            queries.reshape(block_count, block_rows, head_count, head_width),
            grads_low.reshape(block_count, block_rows, head_count, head_width),
            log_totals.reshape(block_count, block_rows, head_count),
            query_index.reshape(block_count, block_rows),
            query_seg.reshape(block_count, block_rows),
        ),
    )
    return (query_grad.reshape(query_total, head_count, head_width), key_grad, value_grad)


def local(
    tokens,
    cotangent,
    segment_ids,
    tile_owner_slots,
    weights_low,
    master,
    moment_one,
    moment_two,
    left_basis_set,
    right_basis_set,
    gains,
    gain_moment_one,
    gain_moment_two,
):
    grp_count = lax.axis_size("grp")
    seq_count = lax.axis_size("seq")
    grp_here = lax.axis_index("grp")
    rows_here = tokens.shape[0]
    slots_here, rows_block, tile_width = weights_low.shape
    query_cols = NH * HD
    value_end = query_cols + 2 * HD
    output_end = value_end + MODEL_WIDTH
    attn_tiles = output_end // tile_width
    hidden_tiles = FF // tile_width
    share = -(-hidden_tiles // grp_count)
    share_cols = share * tile_width
    sub_rows = rows_block // grp_count
    local_index = lax.axis_index("seq") * rows_here + jnp.arange(rows_here, dtype=jnp.int32)
    local_place = local_index % SEQLEN
    plane_tiles = lax.all_gather(weights_low, "grp", axis=0, tiled=True)
    hidden_ids = grp_here * share + jnp.arange(share, dtype=jnp.int32)
    real = hidden_ids < hidden_tiles
    hidden_ids = jnp.minimum(hidden_ids, hidden_tiles - 1)
    feed_ids = (
        attn_tiles + jnp.arange(3, dtype=jnp.int32)[:, None] * hidden_tiles + hidden_ids[None, :]
    ).reshape(-1)
    attn_rows = lax.dynamic_slice_in_dim(plane_tiles, grp_here * sub_rows, sub_rows, axis=1)
    attn_rows = jnp.transpose(attn_rows[tile_owner_slots[:attn_tiles]], (1, 0, 2)).reshape(
        sub_rows, output_end
    )
    attn_weights = lax.all_gather(attn_rows, "seq", axis=0, tiled=False)
    attn_weights = lax.all_gather(attn_weights, "grp", axis=1, tiled=True).reshape(
        MODEL_WIDTH, output_end
    )
    feed_tiles = jnp.where(
        jnp.tile(real, 3)[:, None, None], plane_tiles[tile_owner_slots[feed_ids]], 0
    )
    feed_rows = jnp.transpose(feed_tiles, (1, 0, 2)).reshape(rows_block, 3 * share_cols)
    feed_weights = lax.all_gather(feed_rows, "seq", axis=0, tiled=True)
    cot_plane = lax.all_gather(cotangent, "grp", axis=0, tiled=True)
    tok_float = tokens.astype(jnp.float32)
    inverse_one = lax.rsqrt(jnp.mean(tok_float * tok_float, axis=-1, keepdims=True) + NORM_EPS)
    normed = (tok_float * inverse_one * gains[0]).astype(jnp.bfloat16)
    projected = jnp.dot(normed, attn_weights[:, :value_end], preferred_element_type=jnp.float32)
    queries = rotate(projected[:, :query_cols].reshape(rows_here, NH, HD), local_place, 1.0).astype(
        jnp.bfloat16
    )
    key_rows = (
        rotate(
            projected[:, query_cols : query_cols + HD].reshape(rows_here, 1, HD), local_place, 1.0
        )
        .reshape(rows_here, HD)
        .astype(jnp.bfloat16)
    )
    value_rows = projected[:, query_cols + HD : value_end].astype(jnp.bfloat16)
    all_pairs = lax.all_gather(
        jnp.concatenate([key_rows, value_rows], axis=1), "seq", axis=0, tiled=True
    )
    all_keys = all_pairs[:, :HD]
    all_values = all_pairs[:, HD:]
    all_segs = lax.all_gather(segment_ids, "seq", axis=0, tiled=True)
    group_index = jnp.arange(all_keys.shape[0], dtype=jnp.int32)
    group_place = group_index % SEQLEN
    heads_here = NH // seq_count
    head_queries = lax.all_to_all(
        queries.reshape(rows_here, query_cols), "seq", split_axis=1, concat_axis=0, tiled=True
    ).reshape(-1, heads_here, HD)
    head_context, log_totals = attend(
        head_queries, all_keys, all_values, group_index, all_segs, group_index, all_segs
    )
    context = lax.all_to_all(
        head_context.reshape(-1, heads_here * HD).astype(jnp.bfloat16),
        "seq",
        split_axis=0,
        concat_axis=1,
        tiled=True,
    )
    branch = jnp.dot(context, attn_weights[:, value_end:], preferred_element_type=jnp.float32)
    hidden = tok_float + branch
    inverse_two = lax.rsqrt(jnp.mean(hidden * hidden, axis=-1, keepdims=True) + NORM_EPS)
    normed_two = (hidden * inverse_two * gains[1]).astype(jnp.bfloat16)
    normed_plane = lax.all_gather(normed_two, "grp", axis=0, tiled=True)
    gating_weights = feed_weights[:, : 2 * share_cols]
    down_weights = feed_weights[:, 2 * share_cols :]
    gate_up = jnp.dot(normed_plane, gating_weights, preferred_element_type=jnp.float32)
    gate = gate_up[:, :share_cols]
    upper = gate_up[:, share_cols:]
    sigmoid_gate = jax.nn.sigmoid(gate)
    silu_gate = jax.nn.silu(gate)
    activated = (silu_gate * upper).astype(jnp.bfloat16)
    act_grad = jnp.dot(cot_plane, down_weights, preferred_element_type=jnp.float32)
    gate_grad = (act_grad * upper * sigmoid_gate * (1.0 + gate * (1.0 - sigmoid_gate))).astype(
        jnp.bfloat16
    )
    up_grad = (act_grad * silu_gate).astype(jnp.bfloat16)
    gating_grad = jnp.concatenate([gate_grad, up_grad], axis=1)
    norm_two_grad = lax.psum_scatter(
        times_transpose(gating_grad, gating_weights).astype(jnp.bfloat16),
        "grp",
        scatter_dimension=0,
        tiled=True,
    ).astype(jnp.float32)
    feed_grads = jnp.concatenate(
        [contract(normed_plane, gating_grad), contract(cot_plane, activated)], axis=1
    ).astype(jnp.bfloat16)
    feed_grads = lax.psum_scatter(feed_grads, "seq", scatter_dimension=0, tiled=True)
    feed_grads = jnp.transpose(feed_grads.reshape(rows_block, 3 * share, tile_width), (1, 0, 2))
    feed_grads = lax.all_gather(feed_grads, "grp", axis=0, tiled=True)
    feed_out = lax.psum_scatter(
        times_transpose(activated, down_weights).astype(jnp.bfloat16),
        "grp",
        scatter_dimension=0,
        tiled=True,
    ).astype(jnp.float32)
    block_out = (hidden + feed_out).astype(jnp.bfloat16)
    out_grad = cotangent.astype(jnp.float32)
    gain_two_term = jnp.sum(norm_two_grad * hidden * inverse_two, axis=0)
    hidden_grad = (
        out_grad
        + inverse_two * gains[1] * norm_two_grad
        - hidden
        * inverse_two**3
        * jnp.mean(hidden * gains[1] * norm_two_grad, axis=-1, keepdims=True)
    )
    branch_grad = hidden_grad.astype(jnp.bfloat16)
    context_grad = times_transpose(branch_grad, attn_weights[:, value_end:]).astype(jnp.bfloat16)
    head_grads = lax.all_to_all(
        context_grad, "seq", split_axis=1, concat_axis=0, tiled=True
    ).reshape(-1, heads_here, HD)

    def reduce_rows(part):
        cols = part.shape[1]
        blocks = jnp.transpose(
            part.astype(jnp.bfloat16).reshape(seq_count, grp_count, sub_rows, cols), (1, 0, 2, 3)
        ).reshape(grp_count * seq_count * sub_rows, cols)
        summed = lax.psum_scatter(blocks, ("grp", "seq"), scatter_dimension=0, tiled=True)
        return lax.all_gather(summed, "grp", axis=0, tiled=True)

    out_grads = reduce_rows(contract(context, branch_grad))
    head_query_grad, key_part, value_part = attend_back(
        head_queries,
        all_keys,
        all_values,
        head_grads,
        log_totals,
        group_index,
        all_segs,
        group_index,
        all_segs,
    )
    turned_query = (
        rotate(head_query_grad, group_place, -1.0).reshape(-1, heads_here * HD).astype(jnp.bfloat16)
    )
    query_grad = lax.all_to_all(turned_query, "seq", split_axis=0, concat_axis=1, tiled=True)
    key_part = rotate(key_part[:, None, :], group_place, -1.0)[:, 0, :]
    pair_grad = lax.psum_scatter(
        jnp.concatenate([key_part, value_part], axis=1), "seq", scatter_dimension=0, tiled=True
    )
    projected_grad = jnp.concatenate([query_grad, pair_grad.astype(jnp.bfloat16)], axis=1)
    in_grads = reduce_rows(contract(normed, projected_grad))
    norm_one_grad = times_transpose(projected_grad, attn_weights[:, :value_end])
    gain_one_term = jnp.sum(norm_one_grad * tok_float * inverse_one, axis=0)
    input_grad = (
        hidden_grad
        + inverse_one * gains[0] * norm_one_grad
        - tok_float
        * inverse_one**3
        * jnp.mean(tok_float * gains[0] * norm_one_grad, axis=-1, keepdims=True)
    )
    gain_grads = lax.psum(jnp.stack([gain_one_term, gain_two_term]), ("grp", "seq"))
    tile_count = tile_owner_slots.shape[0]
    tile_of_slot = (
        jnp.full((grp_count * slots_here,), tile_count, jnp.int32)
        .at[tile_owner_slots]
        .set(jnp.arange(tile_count, dtype=jnp.int32))
    )
    tiles_here = lax.dynamic_slice_in_dim(tile_of_slot, grp_here * slots_here, slots_here)
    attn_grads = jnp.transpose(
        jnp.concatenate([in_grads, out_grads], axis=1).reshape(rows_block, attn_tiles, tile_width),
        (1, 0, 2),
    )
    feed_at = jnp.clip(tiles_here - attn_tiles, 0, 3 * hidden_tiles - 1)
    which, column = (feed_at // hidden_tiles, feed_at % hidden_tiles)
    feed_at = column // share * (3 * share) + which * share + column % share
    picked = jnp.where(
        (tiles_here < attn_tiles)[:, None, None],
        attn_grads[jnp.minimum(tiles_here, attn_tiles - 1)],
        feed_grads[feed_at],
    )
    reduced_sum = jnp.where((tiles_here < tile_count)[:, None, None], picked, 0).astype(jnp.float32)
    turned = jnp.einsum("zji,zjc->zic", left_basis_set, reduced_sum)
    turned = jnp.einsum("zic,zcd->zid", turned, right_basis_set)
    new_one = BETA_ONE * moment_one + (1.0 - BETA_ONE) * turned
    new_two = BETA_TWO * moment_two + (1.0 - BETA_TWO) * turned * turned
    scaled = new_one / (jnp.sqrt(new_two) + ADAM_EPS)
    restored = jnp.einsum("zij,zjd->zid", left_basis_set, scaled)
    restored = jnp.einsum("zid,zed->zie", restored, right_basis_set)
    new_master = master * (1.0 - LEARN_RATE * WEIGHT_DECAY) - LEARN_RATE * restored
    gain_one = BETA_ONE * gain_moment_one + (1.0 - BETA_ONE) * gain_grads
    gain_two = BETA_TWO * gain_moment_two + (1.0 - BETA_TWO) * gain_grads * gain_grads
    new_gains = gains - GAIN_RATE * gain_one / (jnp.sqrt(gain_two) + ADAM_EPS)
    return (
        block_out,
        input_grad,
        new_master,
        new_one,
        new_two,
        gain_grads,
        new_gains,
        gain_one,
        gain_two,
    )


def solution(mesh):
    return jax.shard_map(
        local,
        mesh=mesh,
        in_specs=(
            P(("grp", "seq"), None),
            P(("grp", "seq"), None),
            P(("grp", "seq")),
            P(),
            P("grp", "seq", None),
            P("grp", "seq", None),
            P("grp", "seq", None),
            P("grp", "seq", None),
            P("grp", "seq", None),
            P("grp", "seq", None),
            P(),
            P(),
            P(),
        ),
        out_specs=(
            P(("grp", "seq"), None),
            P(("grp", "seq"), None),
            P("grp", "seq", None),
            P("grp", "seq", None),
            P("grp", "seq", None),
            P(),
            P(),
            P(),
            P(),
        ),
        check_vma=False,
    )
```

profile of v0, /device:TPU:0, one launch (start us, length us, event | category | flops | bytes accessed | tf_op | source)
XLA Modules:
  0.0 1731.6 jit_solution(6610942294189539147)
XLA Ops:
  8.7 116.0 %all-gather.11.cloned.1.call-done = bf16[168,512,128]{2,1,0:T(8,128)(2,1)} async-done(((bf16[21,512,128]{2,1,0:T(8,128)(2,1)}), bf16[168,512,128]{2,1,0:T(8,128)(2,1)}) %all-gather.11.cloned.1.call-update) | async-done | bytes 22020112 | tf_op jit(solution)/shard_map/all_gather | solution.py:172
  134.4 48.4 %all-gather.13.cloned.1.call-done = bf16[4,64,4352]{2,1,0:T(8,128)(2,1)} async-done(((bf16[1,64,4352]{2,1,0:T(8,128)(2,1)}), bf16[4,64,4352]{2,1,0:T(8,128)(2,1)}) %all-gather.13.cloned.1.call-update) | async-done | bytes 2228240 | tf_op jit(solution)/shard_map/all_gather | solution.py:183
  204.3 73.6 %all-gather.15.cloned.1.call-done = bf16[4,512,4352]{2,1,0:T(8,128)(2,1)} async-done(((bf16[4,64,4352]{2,1,0:T(8,128)(2,1)}), bf16[4,512,4352]{2,1,0:T(8,128)(2,1)}) %all-gather.15.cloned.1.call-update) | async-done | bytes 17825808 | tf_op jit(solution)/shard_map/all_gather | solution.py:184
  296.3 40.8 %all-gather = s32[4,1,256]{2,1,0:T(1,128)S(1)} all-gather(s32[1,1,256]{2,1,0:T(1,128)} %bitcast.336), channel_id=1, replica_groups=mesh['grp'=8,'seq'=4] {'seq'}, dimensions={0}, use_global_device_ids=true | all-gather | bytes 5120 | tf_op jit(solution)/shard_map/all_gather | solution.py:213
  339.6 43.2 %all_gather.37 = bf16[1024,256]{0,1:T(8,128)(2,1)S(1)} all-gather(bf16[256,256]{0,1:T(8,128)(2,1)S(1)} %pad_maximum_fusion.11), channel_id=1, replica_groups=mesh['grp'=8,'seq'=4] {'seq'}, dimensions={0}, use_global_device_ids=true | all-gather | bytes 655360 | tf_op jit(solution)/shard_map/all_gather | solution.py:208
  388.0 17.3 while.36
  410.6 59.3 %all_to_all.61 = bf16[4,256,512]{2,1,0:T(8,128)(2,1)} all-to-all(bf16[4,256,512]{2,1,0:T(8,128)(2,1)} %convert_element_type.137), channel_id=1, replica_groups=mesh['grp'=8,'seq'=4] {'seq'}, dimensions={0} | all-to-all | bytes 2097152 | tf_op jit(solution)/shard_map/all_to_all | solution.py:223
  481.9 18.0 %all-gather.19.cloned.1.call-done = bf16[2048,2304]{0,1:T(8,128)(2,1)} async-done(((bf16[512,2304]{0,1:T(8,128)(2,1)}), bf16[2048,2304]{0,1:T(8,128)(2,1)}) %all-gather.19.cloned.1.call-update) | async-done | bytes 9437200 | tf_op jit(solution)/shard_map/all_gather | solution.py:191
  499.8 54.9 %all-gather.17.cloned.1.call-done = bf16[2048,2048]{1,0:T(8,128)(2,1)} async-done(((bf16[256,2048]{1,0:T(8,128)(2,1)}), bf16[2048,2048]{1,0:T(8,128)(2,1)}) %all-gather.17.cloned.1.call-update) | async-done | bytes 8388624 | tf_op jit(solution)/shard_map/all_gather | solution.py:234
  554.8 19.0 %fusion.95 = f32[2048,1536]{0,1:T(8,128)} fusion(bf16[2048,2048]{1,0:T(8,128)(2,1)} %all-gather.17.cloned.1.call-done, bf16[2048,2304]{0,1:T(8,128)(2,1)} %all-gather.19.cloned.1.call-done), kind=kOutput, calls=%fused_computation.134 | convolution fusion | flops 12884901888 | bytes 27262976 | tf_op jit(solution)/shard_map/dot_general | solution.py:237
  573.7 37.2 %all-gather.21.cloned.1.call-done = bf16[2048,2048]{1,0:T(8,128)(2,1)} async-done(((bf16[256,2048]{1,0:T(8,128)(2,1)}), bf16[2048,2048]{1,0:T(8,128)(2,1)}) %all-gather.21.cloned.1.call-update) | async-done | bytes 8388624 | tf_op jit(solution)/shard_map/all_gather | solution.py:192
  610.9 16.7 fusion.91
  629.3 18.7 %convolution_convert_fusion.3 = bf16[2048,2048]{1,0:T(8,128)(2,1)} fusion(bf16[2048,2304]{0,1:T(8,128)(2,1)} %all-gather.19.cloned.1.call-done, bf16[2048,768]{0,1:T(8,128)(2,1)} %get-tuple-element.680, bf16[2048,768]{0,1:T(8,128)(2,1)S(1)} %get-tuple-element.679), kind=kOutput, calls=%fused_computation.117 | convolution fusion | flops 12901679104 | bytes 20971520 | tf_op jit(solution)/shard_map/dot_general | solution.py:51
  648.1 11.9 convolution_convert_fusion.4
  660.0 59.5 %reduce-scatter.9.cloned.1.call-done = bf16[256,2048]{1,0:T(8,128)(2,1)} async-done(((bf16[2048,2048]{1,0:T(8,128)(2,1)}), bf16[256,2048]{1,0:T(8,128)(2,1)}) %reduce-scatter.9.cloned.1.call-update) | async-done | bytes 1048592 | tf_op jit(solution)/shard_map/reduce_scatter | solution.py:249
  722.5 72.2 %reduce-scatter.7.cloned.1.call-done = bf16[256,2048]{1,0:T(8,128)(2,1)} async-done(((bf16[2048,2048]{1,0:T(8,128)(2,1)}), bf16[256,2048]{1,0:T(8,128)(2,1)}) %reduce-scatter.7.cloned.1.call-update) | async-done | bytes 1048592 | tf_op jit(solution)/shard_map/reduce_scatter | solution.py:261
  811.1 25.8 %all-to-all-done.2 = bf16[256,4,512]{2,0,1:T(8,128)(2,1)} async-done(((bf16[256,4,512]{2,0,1:T(8,128)(2,1)}), bf16[256,4,512]{2,0,1:T(8,128)(2,1)}, u32[]{:S(2)}, u32[]{:S(2)}) %all-to-all-start.2) | async-done | bytes 1048608 | tf_op jit(solution)/shard_map/all_to_all | solution.py:279
  839.5 123.5 %while.37 = (s32[]{:T(128)}, f32[1024,128]{1,0:T(8,128)}, f32[1024,128]{1,0:T(8,128)}, f32[2,512,4,128]{3,1,0,2:T(8,128)}, s32[2,512]{1,0:T(2,128)S(1)}, /*index...) while((s32[]{:T(128)}, f32[1024,128]{1,0:T(8,128)}, ...), condition=%wide.region_11.12_spmd.clone.clone, body=%wide.region_9.11_spmd.clone.clone.sunk | while | flops 2742048256 | bytes 106783928 | solution.py:128
  850.3 22.8 %fusion.228 = f32[2,512,4,128]{3,1,0,2:T(8,128)} fusion(f32[2,512,4,128]{3,1,0,2:T(8,128)} %get-tuple-element.900, s32[]{:T(128)} %get-tuple-element.897, f32[512,4,1024]{2,0,1:T(8,128)} %fusion.223, f32[512,4,1024]{2,0,1:T(8,128)} %fusion.224, f32[4,512]{1,0:T(4,128)S(1)} %dynamic-slice_bitcast_fusion.2, pred[512,1024]{1,0:T(8,128)(4,1)} %fusion.225, ...), kind=kOutput, calls=%fused_computation.67.clone.1 | convolution fusion | flops 559942656 | bytes 35930624 | tf_op jit(solution)/shard_map/while/body/eval_jaxpr/hqk,kd->qhd/dot_general | solution.py:113
  873.1 21.3 %fusion.226 = f32[1024,128]{1,0:T(8,128)} fusion(f32[512,4,1024]{2,0,1:T(8,128)} %fusion.223, f32[512,4,1024]{2,0,1:T(8,128)} %fusion.224, f32[4,512]{1,0:T(4,128)S(1)} %dynamic-slice_bitcast_fusion.2, pred[512,1024]{1,0:T(8,128)(4,1)} %fusion.225, f32[1024,128]{1,0:T(8,128)} %get-tuple-element.898, ...), kind=kOutput, calls=%fused_computation.70.clone.1 | convolution fusion | flops 560204800 | bytes 36192768 | tf_op jit(solution)/shard_map/while/body/eval_jaxpr/hqk,qhd->kd/dot_general | solution.py:116
  912.0 22.8 %fusion.228 = f32[2,512,4,128]{3,1,0,2:T(8,128)} fusion(f32[2,512,4,128]{3,1,0,2:T(8,128)} %get-tuple-element.900, s32[]{:T(128)} %get-tuple-element.897, f32[512,4,1024]{2,0,1:T(8,128)} %fusion.223, f32[512,4,1024]{2,0,1:T(8,128)} %fusion.224, f32[4,512]{1,0:T(4,128)S(1)} %dynamic-slice_bitcast_fusion.2, pred[512,1024]{1,0:T(8,128)(4,1)} %fusion.225, ...), kind=kOutput, calls=%fused_computation.67.clone.1 | convolution fusion | flops 559942656 | bytes 35930624 | tf_op jit(solution)/shard_map/while/body/eval_jaxpr/hqk,kd->qhd/dot_general | solution.py:113
  934.8 21.3 %fusion.226 = f32[1024,128]{1,0:T(8,128)} fusion(f32[512,4,1024]{2,0,1:T(8,128)} %fusion.223, f32[512,4,1024]{2,0,1:T(8,128)} %fusion.224, f32[4,512]{1,0:T(4,128)S(1)} %dynamic-slice_bitcast_fusion.2, pred[512,1024]{1,0:T(8,128)(4,1)} %fusion.225, f32[1024,128]{1,0:T(8,128)} %get-tuple-element.898, ...), kind=kOutput, calls=%fused_computation.70.clone.1 | convolution fusion | flops 560204800 | bytes 36192768 | tf_op jit(solution)/shard_map/while/body/eval_jaxpr/hqk,qhd->kd/dot_general | solution.py:116
  977.2 41.2 %all_to_all.62 = bf16[4,256,512]{2,1,0:T(8,128)(2,1)} all-to-all(bf16[4,256,512]{2,1,0:T(8,128)(2,1)} %convert_element_type.151), channel_id=1, replica_groups=mesh['grp'=8,'seq'=4] {'seq'}, dimensions={0} | all-to-all | bytes 2097152 | tf_op jit(solution)/shard_map/all_to_all | solution.py:306
  1062.7 15.9 convolution_convert_fusion.1
  1078.6 11.5 pad_maximum_fusion
  1090.2 79.3 %reduce-scatter.13.cloned.1.call-done = bf16[64,2304]{1,0:T(8,128)(2,1)} async-done(((bf16[2048,2304]{1,0:T(8,128)(2,1)}), bf16[64,2304]{1,0:T(8,128)(2,1)}) %reduce-scatter.13.cloned.1.call-update) | async-done | bytes 294928 | tf_op jit(solution)/shard_map/reduce_scatter | solution.py:288
  1169.6 187.0 %reduce-scatter.15.cloned.1.call-done = bf16[64,2048]{1,0:T(8,128)(2,1)} async-done(((bf16[2048,2048]{1,0:T(8,128)(2,1)}), bf16[64,2048]{1,0:T(8,128)(2,1)}) %reduce-scatter.15.cloned.1.call-update) | async-done | bytes 262160 | tf_op jit(solution)/shard_map/reduce_scatter | solution.py:288
  1356.7 161.1 %reduce-scatter.17.cloned.1.call-done = bf16[512,2304]{0,1:T(8,128)(2,1)} async-done(((bf16[2048,2304]{0,1:T(8,128)(2,1)}), bf16[512,2304]{0,1:T(8,128)(2,1)}) %reduce-scatter.17.cloned.1.call-update) | async-done | bytes 2359312 | tf_op jit(solution)/shard_map/reduce_scatter | solution.py:258
  1534.5 41.6 %psum.7 = f32[2,2048]{1,0:T(2,128)S(1)} all-reduce(f32[2,2048]{1,0:T(2,128)S(1)} %pad_maximum_fusion.12), channel_id=1, replica_groups=mesh['grp'=8,'seq'=4] {'grp','seq'}, use_global_device_ids=true, to_apply=%region_20.21 | all-reduce | flops 4096 | bytes 32768 | tf_op jit(solution)/shard_map/psum | solution.py:322
  1605.0 76.1 %all-gather.27.cloned.1.call-done = bf16[144,512,128]{2,1,0:T(8,128)(2,1)} async-done(((bf16[18,512,128]{2,1,0:T(8,128)(2,1)}), bf16[144,512,128]{2,1,0:T(8,128)(2,1)}) %all-gather.27.cloned.1.call-update) | async-done | bytes 18874384 | tf_op jit(solution)/shard_map/all_gather | solution.py:260
  1690.0 18.5 %fusion.97 = (f32[21,512,128]{2,1,0:T(8,128)}, f32[21,512,128]{2,1,0:T(8,128)}) fusion(f32[21,512,128]{2,1,0:T(8,128)} %param.24, f32[21,512,128]{2,1,0:T(8,128)} %param.23, f32[21,128,128]{2,1,0:T(8,128)S(1)} %copy-done, f32[21,512,512]{2,1,0:T(8,128)} %param.25, bf16[21,512,128]{2,1,0:T(8,128)(2,1)} %gather_fusion.3, ...), kind=kOutput, calls=%fused_computation.136 | convolution fusion | flops 1772617728 | bytes 50921512 | tf_op jit(solution)/shard_map/zic,zcd->zid/dot_general | solution.py:344
  1708.5 16.1 multiply_subtract_fusion
  (235 shorter events, 264.9 us)
Async XLA Ops:
  7.2 1682.9 %copy-start = (f32[21,128,128]{2,1,0:T(8,128)S(1)}, f32[21,128,128]{2,1,0:T(8,128)}, u32[]{:S(2)}) copy-start(f32[21,128,128]{2,1,0:T(8,128)} %param.26) | copy-start | bytes 4128772
  7.2 117.5 %all-gather.11.cloned.1.call-start = ((), (), s32[]{:S(2)}) async-start(), calls=%async_computation.10 | async-start | bytes 24772608 | tf_op jit(solution)/shard_map/all_gather | solution.py:172
  7.9 174.9 %all-gather.13.cloned.1.call-start = ((), (), s32[]{:S(2)}) async-start(), calls=%async_computation.11 | async-start | bytes 2785280 | tf_op jit(solution)/shard_map/all_gather | solution.py:183
  8.7 174.4 %copy-start.1 = (s32[166]{0:T(256)S(1)}, s32[166]{0:T(256)}, u32[]{:S(2)}) copy-start(s32[166]{0:T(256)} %param.20) | copy-start | bytes 1996
  8.7 175.3 %copy-start.7 = (bf16[256,2048]{1,0:T(8,128)(2,1)S(1)}, bf16[256,2048]{1,0:T(8,128)(2,1)}, u32[]{:S(2)}) copy-start(bf16[256,2048]{1,0:T(8,128)(2,1)} %param.17) | copy-start | bytes 3145732
  134.4 143.5 %all-gather.15.cloned.1.call-start = ((), (), s32[]{:S(2)}) async-start(), calls=%async_computation.12 | async-start | bytes 20054016 | tf_op jit(solution)/shard_map/all_gather | solution.py:184
  182.9 317.0 %all-gather.19.cloned.1.call-start = ((), (), s32[]{:S(2)}) async-start(), calls=%async_computation.14 | async-start | bytes 11796480 | tf_op jit(solution)/shard_map/all_gather | solution.py:191
  202.7 136.5 %copy-start.22 = (f32[64]{0:T(128)}, f32[64]{0:T(128)S(1)}, u32[]{:S(2)}) copy-start(f32[64]{0:T(128)S(1)} %multiply_power_fusion) | copy-start | bytes 772
  203.3 80.9 %copy-start.19 = (f32[256]{0:T(256)}, f32[256]{0:T(256)S(1)}, u32[]{:S(2)}) copy-start(f32[256]{0:T(256)S(1)} %get-tuple-element.703) | copy-start | bytes 3076
  204.3 80.0 %copy-start.13 = (f32[1,2048]{1,0:T(1,128)}, f32[1,2048]{1,0:T(1,128)S(1)}, u32[]{:S(2)}) copy-start(f32[1,2048]{1,0:T(1,128)S(1)} %get-tuple-element.697) | copy-start | bytes 24580
  291.7 91.5 %all-to-all-start = ((bf16[256,4,512]{0,2,1:T(8,128)(2,1)}), bf16[256,4,512]{0,2,1:T(8,128)(2,1)S(1)}, u32[]{:S(2)}, u32[]{:S(2)}) async-start(bf16[256,4,512]{0,2,1:T(8,128)(2,1)} %bitcast.5), calls=%async_computation | async-start | bytes 2097152 | tf_op jit(solution)/shard_map/all_to_all | solution.py:217
  296.3 258.4 %all-gather.17.cloned.1.call-start = ((), (), s32[]{:S(2)}) async-start(), calls=%async_computation.13 | async-start | bytes 9437184 | tf_op jit(solution)/shard_map/all_gather | solution.py:234
  481.1 129.9 %all-gather.21.cloned.1.call-start = ((), (), s32[]{:S(2)}) async-start(), calls=%async_computation.16 | async-start | bytes 9437184 | tf_op jit(solution)/shard_map/all_gather | solution.py:192
  481.7 237.9 %reduce-scatter.9.cloned.1.call-start = ((), (), s32[]{:S(2)}) async-start(), calls=%async_computation.17 | async-start | bytes 9437184 | tf_op jit(solution)/shard_map/reduce_scatter | solution.py:249
  648.1 146.6 %reduce-scatter.7.cloned.1.call-start = ((), (), s32[]{:S(2)}) async-start(), calls=%async_computation.15 | async-start | bytes 9437184 | tf_op jit(solution)/shard_map/reduce_scatter | solution.py:261
  806.5 30.4 %all-to-all-start.2 = ((bf16[256,4,512]{2,0,1:T(8,128)(2,1)}), bf16[256,4,512]{2,0,1:T(8,128)(2,1)}, u32[]{:S(2)}, u32[]{:S(2)}) async-start(bf16[256,4,512]{2,0,1:T(8,128)(2,1)} %bitcast.312), calls=%async_computation.4 | async-start | bytes 2097152 | tf_op jit(solution)/shard_map/all_to_all | solution.py:279
  811.1 208.7 %reduce-scatter.11.cloned.1.call-start = ((), (), s32[]{:S(2)}) async-start(), calls=%async_computation.18 | async-start | bytes 1310720 | tf_op jit(solution)/shard_map/reduce_scatter | solution.py:308
  839.5 127.7 %copy-start.23 = (f32[64]{0:T(128)S(1)}, f32[64]{0:T(128)}, u32[]{:S(2)}) copy-start(f32[64]{0:T(128)} %copy-done.22) | copy-start | bytes 772
  971.8 197.8 %reduce-scatter.13.cloned.1.call-start = ((), (), s32[]{:S(2)}) async-start(), calls=%async_computation.19 | async-start | bytes 9732096 | tf_op jit(solution)/shard_map/reduce_scatter | solution.py:288
  974.5 46.6 %copy-start.8 = (bf16[256,2048]{1,0:T(8,128)(2,1)S(1)}, bf16[256,2048]{1,0:T(8,128)(2,1)}, u32[]{:S(2)}) copy-start(bf16[256,2048]{1,0:T(8,128)(2,1)} %param.17) | copy-start | bytes 3145732
  974.5 46.6 %copy-start.14 = (f32[1,2048]{1,0:T(1,128)S(1)}, f32[1,2048]{1,0:T(1,128)}, u32[]{:S(2)}) copy-start(f32[1,2048]{1,0:T(1,128)} %copy-done.13) | copy-start | bytes 24580
  974.5 46.6 %copy-start.20 = (f32[256]{0:T(256)S(1)}, f32[256]{0:T(256)}, u32[]{:S(2)}) copy-start(f32[256]{0:T(256)} %copy-done.19) | copy-start | bytes 3076
  1034.7 321.9 %reduce-scatter.15.cloned.1.call-start = ((), (), s32[]{:S(2)}) async-start(), calls=%async_computation.21 | async-start | bytes 8650752 | tf_op jit(solution)/shard_map/reduce_scatter | solution.py:288
  1051.9 465.9 %reduce-scatter.17.cloned.1.call-start = ((), (), s32[]{:S(2)}) async-start(), calls=%async_computation.23 | async-start | bytes 11796480 | tf_op jit(solution)/shard_map/reduce_scatter | solution.py:258
  1090.1 432.0 %copy-start.2 = (s32[166]{0:T(256)S(1)}, s32[166]{0:T(256)}, u32[]{:S(2)}) copy-start(s32[166]{0:T(256)} %param.20) | copy-start | bytes 1996
  1090.2 491.9 %all-gather.23.cloned.1.call-start = ((), (), s32[]{:S(2)}) async-start(), calls=%async_computation.20 | async-start | bytes 2654208 | tf_op jit(solution)/shard_map/all_gather | solution.py:289
  1169.5 412.5 %all-gather.25.cloned.1.call-start = ((), (), s32[]{:S(2)}) async-start(), calls=%async_computation.22 | async-start | bytes 2359296 | tf_op jit(solution)/shard_map/all_gather | solution.py:289
  1356.6 324.5 %all-gather.27.cloned.1.call-start = ((), (), s32[]{:S(2)}) async-start(), calls=%async_computation.24 | async-start | bytes 21233664 | tf_op jit(solution)/shard_map/all_gather | solution.py:260
  1525.1 51.6 %copy-start.16 = (f32[2,2048]{1,0:T(2,128)S(1)}, f32[2,2048]{1,0:T(2,128)}, u32[]{:S(2)}) copy-start(f32[2,2048]{1,0:T(2,128)} %param.27) | copy-start | bytes 49156
  1525.1 51.6 %copy-start.21 = (f32[2,2048]{1,0:T(2,128)S(1)}, f32[2,2048]{1,0:T(2,128)}, u32[]{:S(2)}) copy-start(f32[2,2048]{1,0:T(2,128)} %param.28) | copy-start | bytes 49156
  1600.1 90.0 %copy-start.24 = (pred[21]{0:T(512)(128)(4,1)S(1)}, pred[21]{0:T(512)(128)(4,1)}, u32[]{:S(2)}) copy-start(pred[21]{0:T(512)(128)(4,1)} %get-tuple-element.671) | copy-start | bytes 67
  1600.1 90.0 %copy-start.25 = (pred[21]{0:T(512)(128)(4,1)S(1)}, pred[21]{0:T(512)(128)(4,1)}, u32[]{:S(2)}) copy-start(pred[21]{0:T(512)(128)(4,1)} %broadcast_compare_fusion) | copy-start | bytes 67
  (15 other events, 98.3 us)
Sparse Core Ops, SparseCore 0:
  9.9 114.7 all-gather.10
  134.5 48.3 all-gather.12
  184.8 93.1 all-gather.14
  279.9 219.8 all-gather.18
  502.1 52.5 all-gather.16
  556.5 54.3 all-gather.20
  648.2 71.2 reduce-scatter.8
  723.4 71.2 reduce-scatter.6
  971.9 35.7 reduce-scatter.10
  1034.8 134.6 reduce-scatter.12
  1171.8 184.7 reduce-scatter.14
  1358.8 158.9 reduce-scatter.16
  1519.7 30.3 all-gather.22
  1551.9 28.3 all-gather.24
  1582.5 98.5 all-gather.26
where the time goes:
time: 1740 us; the launch traced here: 1730 us
  waiting for transfers between devices  1010 us (58%)
  matrix products  299 us (17%)
  blocking collectives  226 us (13%)
  local copies, waits for them, and re-layouts  112 us (6%)
  other arithmetic  59.6 us (3%)
    reduce_scatter x2, waiting for transfers between devices, reduce_rows(): lax.psum_scatter(blocks, ('grp', 'seq'), scatter_dimension=0, tiled=True)  266 us
    reduce_scatter x1, waiting for transfers between devices, local(): lax.psum_scatter(feed_grads, 'seq', scatter_dimension=0, tiled=True)  161 us
    all_gather x1, waiting for transfers between devices, local(): plane_tiles = lax.all_gather(weights_low, 'grp', axis=0, tiled=True)  116 us
    all_gather x1, waiting for transfers between devices, local(): feed_grads = lax.all_gather(feed_grads, 'grp', axis=0, tiled=True)  76.1 us
    all_gather x1, waiting for transfers between devices, local(): lax.all_gather(attn_weights, 'grp', axis=1, tiled=True)  73.6 us
    reduce_scatter x1, waiting for transfers between devices, local(): lax.psum_scatter(times_transpose(activated, down_weights).astype(jnp.bflo...  72.2 us
    reduce_scatter x1, waiting for transfers between devices, local(): lax.psum_scatter(times_transpose(gating_grad, gating_weights).astype(jnp....  59.5 us
    all_to_all x1, blocking collectives, local(): lax.all_to_all(head_context.reshape(-1, heads_here * HD).astype(jnp.bfloa...  59.3 us
  transfers between devices with their start and end apart: 17, of which 13 were waited for; matrix products, arithmetic and copies ran while one was open for 12% of the time, Pallas kernels for 0%

commit v1 on v0

--- a/solution.py
+++ b/solution.py
@@ -319,7 +319,9 @@
         * inverse_one**3
         * jnp.mean(tok_float * gains[0] * norm_one_grad, axis=-1, keepdims=True)
     )
-    gain_grads = lax.psum(jnp.stack([gain_one_term, gain_two_term]), ("grp", "seq"))
+    gain_grads = jnp.sum(
+        lax.all_gather(jnp.stack([gain_one_term, gain_two_term]), ("grp", "seq")), axis=0
+    )
     tile_count = tile_owner_slots.shape[0]
     tile_of_slot = (
         jnp.full((grp_count * slots_here,), tile_count, jnp.int32)

time: 1740 us -> 1740 us (level)
  blocking collectives: 226 us -> 263 us
  waiting for transfers between devices: 1010 us -> 974 us
    all_gather x0 -> x1, blocking collectives: none -> 78 us  [local(): lax.all_gather(jnp.stack([gain_one_term, gain_two_term]), ('grp', 'seq'))]
    psum x1 -> x0, blocking collectives: 41.6 us -> none  [local(): lax.psum(jnp.stack([gain_one_term, gain_two_term]), ('grp', 'seq'))]
    all_gather x1, waiting for transfers between devices: 76.1 us -> 39.9 us  [local(): feed_grads = lax.all_gather(feed_grads, 'grp', axis=0, tiled=True)]
where the time goes in v1:
time: 1740 us; the launch traced here: 1730 us
  waiting for transfers between devices  974 us (56%)
  matrix products  299 us (17%)
  blocking collectives  263 us (15%)
  local copies, waits for them, and re-layouts  111 us (6%)
  other arithmetic  60 us (3%)
    reduce_scatter x2, waiting for transfers between devices, reduce_rows(): lax.psum_scatter(blocks, ('grp', 'seq'), scatter_dimension=0, tiled=True)  266 us
    reduce_scatter x1, waiting for transfers between devices, local(): lax.psum_scatter(feed_grads, 'seq', scatter_dimension=0, tiled=True)  161 us
    all_gather x1, waiting for transfers between devices, local(): plane_tiles = lax.all_gather(weights_low, 'grp', axis=0, tiled=True)  116 us
    all_gather x1, blocking collectives, local(): lax.all_gather(jnp.stack([gain_one_term, gain_two_term]), ('grp', 'seq'))  78 us
    all_gather x1, waiting for transfers between devices, local(): lax.all_gather(attn_weights, 'grp', axis=1, tiled=True)  73.6 us
    reduce_scatter x1, waiting for transfers between devices, local(): lax.psum_scatter(times_transpose(activated, down_weights).astype(jnp.bflo...  72.2 us
    reduce_scatter x1, waiting for transfers between devices, local(): lax.psum_scatter(times_transpose(gating_grad, gating_weights).astype(jnp....  59.5 us
    all_to_all x1, blocking collectives, local(): lax.all_to_all(head_context.reshape(-1, heads_here * HD).astype(jnp.bfloa...  59.3 us
  transfers between devices with their start and end apart: 17, of which 13 were waited for; matrix products, arithmetic and copies ran while one was open for 12% of the time, Pallas kernels for 0%

profile of v1, /device:TPU:0, one launch (start us, length us, event | category | flops | bytes accessed | tf_op | source)
XLA Modules:
  0.0 1732.1 jit_solution(3158003115021907554)
XLA Ops:
  8.7 116.0 %all-gather.13.cloned.1.call-done = bf16[168,512,128]{2,1,0:T(8,128)(2,1)} async-done(((bf16[21,512,128]{2,1,0:T(8,128)(2,1)}), bf16[168,512,128]{2,1,0:T(8,128)(2,1)}) %all-gather.13.cloned.1.call-update) | async-done | bytes 22020112 | tf_op jit(solution)/shard_map/all_gather | solution.py:172
  134.4 48.4 %all-gather.15.cloned.1.call-done = bf16[4,64,4352]{2,1,0:T(8,128)(2,1)} async-done(((bf16[1,64,4352]{2,1,0:T(8,128)(2,1)}), bf16[4,64,4352]{2,1,0:T(8,128)(2,1)}) %all-gather.15.cloned.1.call-update) | async-done | bytes 2228240 | tf_op jit(solution)/shard_map/all_gather | solution.py:183
  204.3 73.6 %all-gather.17.cloned.1.call-done = bf16[4,512,4352]{2,1,0:T(8,128)(2,1)} async-done(((bf16[4,64,4352]{2,1,0:T(8,128)(2,1)}), bf16[4,512,4352]{2,1,0:T(8,128)(2,1)}) %all-gather.17.cloned.1.call-update) | async-done | bytes 17825808 | tf_op jit(solution)/shard_map/all_gather | solution.py:184
  296.3 40.8 %all-gather.1 = s32[4,1,256]{2,1,0:T(1,128)S(1)} all-gather(s32[1,1,256]{2,1,0:T(1,128)} %bitcast.338), channel_id=1, replica_groups=mesh['grp'=8,'seq'=4] {'seq'}, dimensions={0}, use_global_device_ids=true | all-gather | bytes 5120 | tf_op jit(solution)/shard_map/all_gather | solution.py:213
  339.6 43.2 %all_gather.43 = bf16[1024,256]{0,1:T(8,128)(2,1)S(1)} all-gather(bf16[256,256]{0,1:T(8,128)(2,1)S(1)} %pad_maximum_fusion.11), channel_id=1, replica_groups=mesh['grp'=8,'seq'=4] {'seq'}, dimensions={0}, use_global_device_ids=true | all-gather | bytes 655360 | tf_op jit(solution)/shard_map/all_gather | solution.py:208
  388.0 17.3 while.36
  410.6 59.3 %all_to_all.61 = bf16[4,256,512]{2,1,0:T(8,128)(2,1)} all-to-all(bf16[4,256,512]{2,1,0:T(8,128)(2,1)} %convert_element_type.137), channel_id=1, replica_groups=mesh['grp'=8,'seq'=4] {'seq'}, dimensions={0} | all-to-all | bytes 2097152 | tf_op jit(solution)/shard_map/all_to_all | solution.py:223
  481.9 17.9 %all-gather.21.cloned.1.call-done = bf16[2048,2304]{0,1:T(8,128)(2,1)} async-done(((bf16[512,2304]{0,1:T(8,128)(2,1)}), bf16[2048,2304]{0,1:T(8,128)(2,1)}) %all-gather.21.cloned.1.call-update) | async-done | bytes 9437200 | tf_op jit(solution)/shard_map/all_gather | solution.py:191
  499.8 54.9 %all-gather.19.cloned.1.call-done = bf16[2048,2048]{1,0:T(8,128)(2,1)} async-done(((bf16[256,2048]{1,0:T(8,128)(2,1)}), bf16[2048,2048]{1,0:T(8,128)(2,1)}) %all-gather.19.cloned.1.call-update) | async-done | bytes 8388624 | tf_op jit(solution)/shard_map/all_gather | solution.py:234
  554.8 19.1 %fusion.95 = f32[2048,1536]{0,1:T(8,128)} fusion(bf16[2048,2048]{1,0:T(8,128)(2,1)} %all-gather.19.cloned.1.call-done, bf16[2048,2304]{0,1:T(8,128)(2,1)} %all-gather.21.cloned.1.call-done), kind=kOutput, calls=%fused_computation.134 | convolution fusion | flops 12884901888 | bytes 27262976 | tf_op jit(solution)/shard_map/dot_general | solution.py:237
  573.9 37.1 %all-gather.23.cloned.1.call-done = bf16[2048,2048]{1,0:T(8,128)(2,1)} async-done(((bf16[256,2048]{1,0:T(8,128)(2,1)}), bf16[2048,2048]{1,0:T(8,128)(2,1)}) %all-gather.23.cloned.1.call-update) | async-done | bytes 8388624 | tf_op jit(solution)/shard_map/all_gather | solution.py:192
  610.9 16.7 fusion.91
  629.3 18.7 %convolution_convert_fusion.3 = bf16[2048,2048]{1,0:T(8,128)(2,1)} fusion(bf16[2048,2304]{0,1:T(8,128)(2,1)} %all-gather.21.cloned.1.call-done, bf16[2048,768]{0,1:T(8,128)(2,1)} %get-tuple-element.680, bf16[2048,768]{0,1:T(8,128)(2,1)S(1)} %get-tuple-element.679), kind=kOutput, calls=%fused_computation.117 | convolution fusion | flops 12901679104 | bytes 20971520 | tf_op jit(solution)/shard_map/dot_general | solution.py:51
  648.1 11.9 convolution_convert_fusion.4
  660.0 59.5 %reduce-scatter.9.cloned.1.call-done = bf16[256,2048]{1,0:T(8,128)(2,1)} async-done(((bf16[2048,2048]{1,0:T(8,128)(2,1)}), bf16[256,2048]{1,0:T(8,128)(2,1)}) %reduce-scatter.9.cloned.1.call-update) | async-done | bytes 1048592 | tf_op jit(solution)/shard_map/reduce_scatter | solution.py:249
  722.5 72.2 %reduce-scatter.7.cloned.1.call-done = bf16[256,2048]{1,0:T(8,128)(2,1)} async-done(((bf16[2048,2048]{1,0:T(8,128)(2,1)}), bf16[256,2048]{1,0:T(8,128)(2,1)}) %reduce-scatter.7.cloned.1.call-update) | async-done | bytes 1048592 | tf_op jit(solution)/shard_map/reduce_scatter | solution.py:261
  811.1 25.8 %all-to-all-done.2 = bf16[256,4,512]{2,0,1:T(8,128)(2,1)} async-done(((bf16[256,4,512]{2,0,1:T(8,128)(2,1)}), bf16[256,4,512]{2,0,1:T(8,128)(2,1)}, u32[]{:S(2)}, u32[]{:S(2)}) %all-to-all-start.2) | async-done | bytes 1048608 | tf_op jit(solution)/shard_map/all_to_all | solution.py:279
  839.5 123.4 %while.37 = (s32[]{:T(128)}, f32[1024,128]{1,0:T(8,128)}, f32[1024,128]{1,0:T(8,128)}, f32[2,512,4,128]{3,1,0,2:T(8,128)}, s32[2,512]{1,0:T(2,128)S(1)}, /*index...) while((s32[]{:T(128)}, f32[1024,128]{1,0:T(8,128)}, ...), condition=%wide.region_11.12_spmd.clone.clone, body=%wide.region_9.11_spmd.clone.clone.sunk | while | flops 2742048256 | bytes 106783928 | solution.py:128
  850.3 22.8 %fusion.228 = f32[2,512,4,128]{3,1,0,2:T(8,128)} fusion(f32[2,512,4,128]{3,1,0,2:T(8,128)} %get-tuple-element.900, s32[]{:T(128)} %get-tuple-element.897, f32[512,4,1024]{2,0,1:T(8,128)} %fusion.223, f32[512,4,1024]{2,0,1:T(8,128)} %fusion.224, f32[4,512]{1,0:T(4,128)S(1)} %dynamic-slice_bitcast_fusion.2, pred[512,1024]{1,0:T(8,128)(4,1)} %fusion.225, ...), kind=kOutput, calls=%fused_computation.67.clone.1 | convolution fusion | flops 559942656 | bytes 35930624 | tf_op jit(solution)/shard_map/while/body/eval_jaxpr/hqk,kd->qhd/dot_general | solution.py:113
  873.2 21.2 %fusion.226 = f32[1024,128]{1,0:T(8,128)} fusion(f32[512,4,1024]{2,0,1:T(8,128)} %fusion.223, f32[512,4,1024]{2,0,1:T(8,128)} %fusion.224, f32[4,512]{1,0:T(4,128)S(1)} %dynamic-slice_bitcast_fusion.2, pred[512,1024]{1,0:T(8,128)(4,1)} %fusion.225, f32[1024,128]{1,0:T(8,128)} %get-tuple-element.898, ...), kind=kOutput, calls=%fused_computation.70.clone.1 | convolution fusion | flops 560204800 | bytes 36192768 | tf_op jit(solution)/shard_map/while/body/eval_jaxpr/hqk,qhd->kd/dot_general | solution.py:116
  911.9 22.9 %fusion.228 = f32[2,512,4,128]{3,1,0,2:T(8,128)} fusion(f32[2,512,4,128]{3,1,0,2:T(8,128)} %get-tuple-element.900, s32[]{:T(128)} %get-tuple-element.897, f32[512,4,1024]{2,0,1:T(8,128)} %fusion.223, f32[512,4,1024]{2,0,1:T(8,128)} %fusion.224, f32[4,512]{1,0:T(4,128)S(1)} %dynamic-slice_bitcast_fusion.2, pred[512,1024]{1,0:T(8,128)(4,1)} %fusion.225, ...), kind=kOutput, calls=%fused_computation.67.clone.1 | convolution fusion | flops 559942656 | bytes 35930624 | tf_op jit(solution)/shard_map/while/body/eval_jaxpr/hqk,kd->qhd/dot_general | solution.py:113
  934.7 21.3 %fusion.226 = f32[1024,128]{1,0:T(8,128)} fusion(f32[512,4,1024]{2,0,1:T(8,128)} %fusion.223, f32[512,4,1024]{2,0,1:T(8,128)} %fusion.224, f32[4,512]{1,0:T(4,128)S(1)} %dynamic-slice_bitcast_fusion.2, pred[512,1024]{1,0:T(8,128)(4,1)} %fusion.225, f32[1024,128]{1,0:T(8,128)} %get-tuple-element.898, ...), kind=kOutput, calls=%fused_computation.70.clone.1 | convolution fusion | flops 560204800 | bytes 36192768 | tf_op jit(solution)/shard_map/while/body/eval_jaxpr/hqk,qhd->kd/dot_general | solution.py:116
  977.1 41.2 %all_to_all.62 = bf16[4,256,512]{2,1,0:T(8,128)(2,1)} all-to-all(bf16[4,256,512]{2,1,0:T(8,128)(2,1)} %convert_element_type.151), channel_id=1, replica_groups=mesh['grp'=8,'seq'=4] {'seq'}, dimensions={0} | all-to-all | bytes 2097152 | tf_op jit(solution)/shard_map/all_to_all | solution.py:306
  1062.7 15.9 convolution_convert_fusion.1
  1078.6 11.5 pad_maximum_fusion
  1090.2 79.0 %reduce-scatter.13.cloned.1.call-done = bf16[64,2304]{1,0:T(8,128)(2,1)} async-done(((bf16[2048,2304]{1,0:T(8,128)(2,1)}), bf16[64,2304]{1,0:T(8,128)(2,1)}) %reduce-scatter.13.cloned.1.call-update) | async-done | bytes 294928 | tf_op jit(solution)/shard_map/reduce_scatter | solution.py:288
  1169.3 187.3 %reduce-scatter.15.cloned.1.call-done = bf16[64,2048]{1,0:T(8,128)(2,1)} async-done(((bf16[2048,2048]{1,0:T(8,128)(2,1)}), bf16[64,2048]{1,0:T(8,128)(2,1)}) %reduce-scatter.15.cloned.1.call-update) | async-done | bytes 262160 | tf_op jit(solution)/shard_map/reduce_scatter | solution.py:288
  1356.6 161.1 %reduce-scatter.17.cloned.1.call-done = bf16[512,2304]{0,1:T(8,128)(2,1)} async-done(((bf16[2048,2304]{0,1:T(8,128)(2,1)}), bf16[512,2304]{0,1:T(8,128)(2,1)}) %reduce-scatter.17.cloned.1.call-update) | async-done | bytes 2359312 | tf_op jit(solution)/shard_map/reduce_scatter | solution.py:258
  1534.4 78.0 %all-gather.2 = f32[32,2,2048]{2,1,0:T(2,128)} all-gather(f32[1,2,2048]{2,1,0:T(2,128)S(1)} %maximum_bitcast_fusion.2), channel_id=2, replica_groups=mesh['grp'=8,'seq'=4] {'grp','seq'}, dimensions={0}, use_global_device_ids=true | all-gather | bytes 540672 | tf_op jit(solution)/shard_map/all_gather | solution.py:323
  1641.7 39.9 %all-gather.29.cloned.1.call-done = bf16[144,512,128]{2,1,0:T(8,128)(2,1)} async-done(((bf16[18,512,128]{2,1,0:T(8,128)(2,1)}), bf16[144,512,128]{2,1,0:T(8,128)(2,1)}) %all-gather.29.cloned.1.call-update) | async-done | bytes 18874384 | tf_op jit(solution)/shard_map/all_gather | solution.py:260
  1690.5 18.5 %fusion.97 = (f32[21,512,128]{2,1,0:T(8,128)}, f32[21,512,128]{2,1,0:T(8,128)}) fusion(f32[21,512,128]{2,1,0:T(8,128)} %param.24, f32[21,512,128]{2,1,0:T(8,128)} %param.23, f32[21,128,128]{2,1,0:T(8,128)S(1)} %copy-done, f32[21,512,512]{2,1,0:T(8,128)} %param.25, bf16[21,512,128]{2,1,0:T(8,128)(2,1)} %gather_fusion.3, ...), kind=kOutput, calls=%fused_computation.136 | convolution fusion | flops 1772617728 | bytes 50921512 | tf_op jit(solution)/shard_map/zic,zcd->zid/dot_general | solution.py:346
  1709.0 16.1 multiply_subtract_fusion
  (238 shorter events, 265.4 us)
Async XLA Ops:
  7.2 1683.3 %copy-start = (f32[21,128,128]{2,1,0:T(8,128)S(1)}, f32[21,128,128]{2,1,0:T(8,128)}, u32[]{:S(2)}) copy-start(f32[21,128,128]{2,1,0:T(8,128)} %param.26) | copy-start | bytes 4128772
  7.2 117.5 %all-gather.13.cloned.1.call-start = ((), (), s32[]{:S(2)}) async-start(), calls=%async_computation.10 | async-start | bytes 24772608 | tf_op jit(solution)/shard_map/all_gather | solution.py:172
  7.9 174.9 %all-gather.15.cloned.1.call-start = ((), (), s32[]{:S(2)}) async-start(), calls=%async_computation.11 | async-start | bytes 2785280 | tf_op jit(solution)/shard_map/all_gather | solution.py:183
  8.7 174.4 %copy-start.1 = (s32[166]{0:T(256)S(1)}, s32[166]{0:T(256)}, u32[]{:S(2)}) copy-start(s32[166]{0:T(256)} %param.20) | copy-start | bytes 1996
  8.7 175.3 %copy-start.7 = (bf16[256,2048]{1,0:T(8,128)(2,1)S(1)}, bf16[256,2048]{1,0:T(8,128)(2,1)}, u32[]{:S(2)}) copy-start(bf16[256,2048]{1,0:T(8,128)(2,1)} %param.17) | copy-start | bytes 3145732
  134.4 143.5 %all-gather.17.cloned.1.call-start = ((), (), s32[]{:S(2)}) async-start(), calls=%async_computation.12 | async-start | bytes 20054016 | tf_op jit(solution)/shard_map/all_gather | solution.py:184
  182.9 317.0 %all-gather.21.cloned.1.call-start = ((), (), s32[]{:S(2)}) async-start(), calls=%async_computation.14 | async-start | bytes 11796480 | tf_op jit(solution)/shard_map/all_gather | solution.py:191
  202.7 136.5 %copy-start.23 = (f32[64]{0:T(128)}, f32[64]{0:T(128)S(1)}, u32[]{:S(2)}) copy-start(f32[64]{0:T(128)S(1)} %multiply_power_fusion) | copy-start | bytes 772
  203.3 81.0 %copy-start.19 = (f32[256]{0:T(256)}, f32[256]{0:T(256)S(1)}, u32[]{:S(2)}) copy-start(f32[256]{0:T(256)S(1)} %get-tuple-element.703) | copy-start | bytes 3076
  204.3 80.0 %copy-start.13 = (f32[1,2048]{1,0:T(1,128)}, f32[1,2048]{1,0:T(1,128)S(1)}, u32[]{:S(2)}) copy-start(f32[1,2048]{1,0:T(1,128)S(1)} %get-tuple-element.697) | copy-start | bytes 24580
  291.7 91.5 %all-to-all-start = ((bf16[256,4,512]{0,2,1:T(8,128)(2,1)}), bf16[256,4,512]{0,2,1:T(8,128)(2,1)S(1)}, u32[]{:S(2)}, u32[]{:S(2)}) async-start(bf16[256,4,512]{0,2,1:T(8,128)(2,1)} %bitcast.5), calls=%async_computation | async-start | bytes 2097152 | tf_op jit(solution)/shard_map/all_to_all | solution.py:217
  296.3 258.4 %all-gather.19.cloned.1.call-start = ((), (), s32[]{:S(2)}) async-start(), calls=%async_computation.13 | async-start | bytes 9437184 | tf_op jit(solution)/shard_map/all_gather | solution.py:234
  481.1 129.8 %all-gather.23.cloned.1.call-start = ((), (), s32[]{:S(2)}) async-start(), calls=%async_computation.16 | async-start | bytes 9437184 | tf_op jit(solution)/shard_map/all_gather | solution.py:192
  481.7 237.7 %reduce-scatter.9.cloned.1.call-start = ((), (), s32[]{:S(2)}) async-start(), calls=%async_computation.17 | async-start | bytes 9437184 | tf_op jit(solution)/shard_map/reduce_scatter | solution.py:249
  648.0 146.6 %reduce-scatter.7.cloned.1.call-start = ((), (), s32[]{:S(2)}) async-start(), calls=%async_computation.15 | async-start | bytes 9437184 | tf_op jit(solution)/shard_map/reduce_scatter | solution.py:261
  806.5 30.4 %all-to-all-start.2 = ((bf16[256,4,512]{2,0,1:T(8,128)(2,1)}), bf16[256,4,512]{2,0,1:T(8,128)(2,1)}, u32[]{:S(2)}, u32[]{:S(2)}) async-start(bf16[256,4,512]{2,0,1:T(8,128)(2,1)} %bitcast.314), calls=%async_computation.4 | async-start | bytes 2097152 | tf_op jit(solution)/shard_map/all_to_all | solution.py:279
  811.1 208.7 %reduce-scatter.11.cloned.1.call-start = ((), (), s32[]{:S(2)}) async-start(), calls=%async_computation.18 | async-start | bytes 1310720 | tf_op jit(solution)/shard_map/reduce_scatter | solution.py:308
  839.5 127.7 %copy-start.24 = (f32[64]{0:T(128)S(1)}, f32[64]{0:T(128)}, u32[]{:S(2)}) copy-start(f32[64]{0:T(128)} %copy-done.23) | copy-start | bytes 772
  971.7 197.5 %reduce-scatter.13.cloned.1.call-start = ((), (), s32[]{:S(2)}) async-start(), calls=%async_computation.19 | async-start | bytes 9732096 | tf_op jit(solution)/shard_map/reduce_scatter | solution.py:288
  974.4 46.6 %copy-start.8 = (bf16[256,2048]{1,0:T(8,128)(2,1)S(1)}, bf16[256,2048]{1,0:T(8,128)(2,1)}, u32[]{:S(2)}) copy-start(bf16[256,2048]{1,0:T(8,128)(2,1)} %param.17) | copy-start | bytes 3145732
  974.5 46.6 %copy-start.14 = (f32[1,2048]{1,0:T(1,128)S(1)}, f32[1,2048]{1,0:T(1,128)}, u32[]{:S(2)}) copy-start(f32[1,2048]{1,0:T(1,128)} %copy-done.13) | copy-start | bytes 24580
  1034.7 321.9 %reduce-scatter.15.cloned.1.call-start = ((), (), s32[]{:S(2)}) async-start(), calls=%async_computation.21 | async-start | bytes 8650752 | tf_op jit(solution)/shard_map/reduce_scatter | solution.py:288
  1051.9 465.9 %reduce-scatter.17.cloned.1.call-start = ((), (), s32[]{:S(2)}) async-start(), calls=%async_computation.23 | async-start | bytes 11796480 | tf_op jit(solution)/shard_map/reduce_scatter | solution.py:258
  1090.1 431.9 %copy-start.2 = (s32[166]{0:T(256)S(1)}, s32[166]{0:T(256)}, u32[]{:S(2)}) copy-start(s32[166]{0:T(256)} %param.20) | copy-start | bytes 1996
  1090.1 528.7 %all-gather.25.cloned.1.call-start = ((), (), s32[]{:S(2)}) async-start(), calls=%async_computation.20 | async-start | bytes 2654208 | tf_op jit(solution)/shard_map/all_gather | solution.py:289
  1169.2 449.6 %all-gather.27.cloned.1.call-start = ((), (), s32[]{:S(2)}) async-start(), calls=%async_computation.22 | async-start | bytes 2359296 | tf_op jit(solution)/shard_map/all_gather | solution.py:289
  1356.6 325.0 %all-gather.29.cloned.1.call-start = ((), (), s32[]{:S(2)}) async-start(), calls=%async_computation.24 | async-start | bytes 21233664 | tf_op jit(solution)/shard_map/all_gather | solution.py:260
  1525.1 89.2 %copy-start.17 = (f32[2,2048]{1,0:T(2,128)S(1)}, f32[2,2048]{1,0:T(2,128)}, u32[]{:S(2)}) copy-start(f32[2,2048]{1,0:T(2,128)} %param.27) | copy-start | bytes 49156
  1525.1 89.3 %copy-start.21 = (f32[2,2048]{1,0:T(2,128)S(1)}, f32[2,2048]{1,0:T(2,128)}, u32[]{:S(2)}) copy-start(f32[2,2048]{1,0:T(2,128)} %param.28) | copy-start | bytes 49156
  1525.1 89.3 %copy-start.22 = (f32[2,2048]{1,0:T(2,128)S(1)}, f32[2,2048]{1,0:T(2,128)}, u32[]{:S(2)}) copy-start(f32[2,2048]{1,0:T(2,128)} %param.29) | copy-start | bytes 49156
  1636.7 53.8 %copy-start.25 = (pred[21]{0:T(512)(128)(4,1)S(1)}, pred[21]{0:T(512)(128)(4,1)}, u32[]{:S(2)}) copy-start(pred[21]{0:T(512)(128)(4,1)} %get-tuple-element.671) | copy-start | bytes 67
  1636.7 53.8 %copy-start.26 = (pred[21]{0:T(512)(128)(4,1)S(1)}, pred[21]{0:T(512)(128)(4,1)}, u32[]{:S(2)}) copy-start(pred[21]{0:T(512)(128)(4,1)} %broadcast_compare_fusion) | copy-start | bytes 67
  (16 other events, 144.1 us)
Sparse Core Ops, SparseCore 0:
  9.9 114.7 all-gather.12
  134.5 48.3 all-gather.14
  184.8 93.1 all-gather.16
  279.9 219.8 all-gather.20
  502.1 52.5 all-gather.18
  556.5 54.3 all-gather.22
  648.1 71.2 reduce-scatter.8
  723.3 71.2 reduce-scatter.6
  971.8 35.7 reduce-scatter.10
  1034.8 134.3 reduce-scatter.12
  1171.5 185.0 reduce-scatter.14
  1358.8 158.9 reduce-scatter.16
  1519.6 30.0 all-gather.24
  1551.5 28.3 all-gather.26
  1582.2 99.3 all-gather.28
